TPU v7x, 256 devices: a whole 4x4x8 slice. The times are simulated.
256 devices in a mesh: chain: 4 (over z_lo, core), mesh: 16 (over z_hi, y), probe: 4 (over x).
Axes of the slice: x: 4, y: 4, z: 8 (z_hi: 4, z_lo: 2; z = z_hi * 2 + z_lo), core: 2. Of those that a mesh axis runs over, the one named last changes fastest.
Arguments:
- signs: int32 [256, 8, 4096], P('probe', 'chain', 'mesh'), may hold values from 0 to 1
- border_signs: int32 [256, 512], P('probe'), may hold values from 0 to 1
- inverse_factors: bfloat16 [8, 4096, 4096], P('chain', 'mesh'), may hold values from -2 to 2, as said below
- couplings: bfloat16 [8, 32, 4, 128, 128], P('chain', 'mesh'), may hold values from -0.15625 to 0.15625
- coupling_cols: int32 [8, 32, 4], P('chain', 'mesh'), may hold values from 0 to 31, all different within a row
- border_rows: bfloat16 [8, 512, 4096], P('chain', None, 'mesh'), may hold values from -0.046875 to 0.046875
- border_inverse: bfloat16 [512, 512], replicated, may hold values from -2 to 2, as said below
Outputs:
- solved: bfloat16 [256, 8, 4096], P('probe', 'chain', 'mesh')
- border_solved: float32 [256, 512], P('probe')
- node_var: float32 [8, 4096], P('chain', 'mesh')
- border_var: float32 [512], replicated
Inputs may be any that keep to these rules, and one draw needn't show every extreme that they name: `inverse_factors`: lower triangular; diagonal entries between 0.5 and 2. `border_inverse`: lower triangular; diagonal entries between 0.5 and 2. `coupling_cols`: the 4 block columns of one block row differ.
All inputs are finite; a program needn't handle non-finite values.
Results may differ from a plain program's by a relative error of at most 0.015.
Values may be sent and summed in bfloat16 or wider, within the bound.
No kernel may reach another device: no remote copies, remote signals or barrier semaphores. Data moves between devices by JAX's collectives and lax.ppermute only.
A program may use at most 64 MiB of HBM per device.

v0:
```python
import jax
import jax.numpy as jnp
from jax import lax
from jax.sharding import PartitionSpec as P


def as_sent(shard):
    return jax.tree.map(lambda a: a.astype(jnp.bfloat16) if a.dtype == jnp.float32 else a, shard)


def shifted(value, axis, steps):
    count = lax.axis_size(axis)
    first, last = (max(0, -steps), min(count, count - steps))
    return lax.ppermute(value, axis, [(source, source + steps) for source in range(first, last)])


def apply_inverse(factor, piece):
    return lax.dot_general(
        piece, factor, (((1,), (1,)), ((), ())), preferred_element_type=jnp.float32
    )


def shards(
    signs, border_signs, inverse_factors, couplings, coupling_cols, border_rows, border_inverse
):
    probes, steps, local = signs.shape
    width = inverse_factors.shape[2]
    block = couplings.shape[3]
    source = (2 * signs - 1).astype(jnp.float32)
    border_source = (2 * border_signs - 1).astype(jnp.float32)

    def coupled_term(prev, step):
        blocks = prev.reshape(probes, width // block, block)[:, coupling_cols[step]]
        term = jnp.einsum(
            "prkc,rkdc->prd", blocks, couplings[step], preferred_element_type=jnp.float32
        )
        return term.reshape(probes, local)

    def sweep(prev):
        outputs = []
        for step in range(steps):
            resid_b = (source[:, step] - coupled_term(prev, step)).astype(jnp.bfloat16)
            solved_now = apply_inverse(
                inverse_factors[step], lax.all_gather(resid_b, "mesh", axis=1, tiled=True)
            ).astype(jnp.bfloat16)
            outputs.append(solved_now)
            if step + 1 < steps:
                prev = lax.all_gather(solved_now, "mesh", axis=1, tiled=True)
        return outputs

    def turn(index, carry):
        prev, unused = carry
        outputs = sweep(prev)
        last = outputs[-1]
        moved = jax.tree.map(
            lambda part, own: part.astype(own.dtype), shifted(as_sent(last), "chain", 1), last
        )
        incoming = jax.tree.map(
            lambda part, own: part.astype(own.dtype),
            lax.all_gather(as_sent(moved), "mesh", axis=1, tiled=True),
            moved,
        )
        return (incoming, jnp.stack(outputs, axis=1))

    start_prev = jnp.zeros((probes, width), jnp.bfloat16)
    start_out = jnp.zeros((probes, steps, local), jnp.bfloat16)
    final_prev, solved = lax.fori_loop(0, lax.axis_size("chain"), turn, (start_prev, start_out))
    partial_border = jnp.zeros((probes, border_rows.shape[1]), jnp.float32)
    for step in range(steps):
        partial_border = partial_border + lax.dot_general(
            solved[:, step],
            border_rows[step],
            (((1,), (1,)), ((), ())),
            preferred_element_type=jnp.float32,
        )
    coupled_border = lax.psum(lax.psum(partial_border, "mesh"), "chain")
    border_resid = (border_source - coupled_border).astype(jnp.bfloat16)
    border_solved = lax.dot_general(
        border_resid, border_inverse, (((1,), (1,)), ((), ())), preferred_element_type=jnp.float32
    )
    total_probes = probes * lax.axis_size("probe")
    node_sums = jnp.sum(jnp.square(solved.astype(jnp.float32)), axis=0)
    node_var = lax.psum(node_sums, "probe") / total_probes
    border_var = lax.psum(jnp.sum(jnp.square(border_solved), axis=0), "probe") / total_probes
    return (solved, border_solved, node_var, border_var)


def solution(mesh):
    return jax.shard_map(
        shards,
        mesh=mesh,
        in_specs=(
            P("probe", "chain", "mesh"),
            P("probe", None),
            P("chain", "mesh", None),
            P("chain", "mesh", None, None, None),
            P("chain", "mesh", None),
            P("chain", None, "mesh"),
            P(),
        ),
        out_specs=(P("probe", "chain", "mesh"), P("probe", None), P("chain", "mesh"), P()),
        check_vma=False,
    )
```

profile of v0, /device:TPU:8, one launch (start us, length us, event | category | flops | bytes accessed | tf_op | source)
XLA Modules:
  0.0 973.0 jit_solution(17167018165982769261)
XLA Ops:
  7.2 1.0 fusion.24
  8.3 728.7 %while.12 = (s32[]{:T(128)}, bf16[64,4096]{1,0:T(8,128)(2,1)S(1)}, bf16[64,2,256]{2,0,1:T(8,128)(2,1)}, f32[64,2,256]{2,0,1:T(8,128)S(1)}, s32[2,2,4]{2,1,0:T(2,...) while((s32[]{:T(128)}, bf16[64,4096]{1,0:T(8,128)(2,1)S(1)}, ...), condition=%wide.region_1.0_spmd, body=%wide.region_0.0_spmd.sunk | while | flops 302123072 | bytes 13771289 | solution.py:67
  8.3 0.8 compare_select_fusion.3
  9.4 0.6 gather_fusion
  10.0 1.1 convolution_bitcast_fusion.4
  11.2 44.7 %all_gather.16 = bf16[64,4096]{1,0:T(8,128)(2,1)S(1)} all-gather(bf16[64,256]{1,0:T(8,128)(2,1)S(1)} %fusion.65), channel_id=1, replica_groups=mesh['chain'=4,'mesh'=16,'probe'=4] {'mesh'}, dimensions={1}, use_global_device_ids=true | all-gather | bytes 557056 | tf_op jit(solution)/shard_map/while/body/eval_jaxpr/all_gather | solution.py:44
  55.9 2.3 fusion.66
  58.2 47.3 %all_gather.17 = bf16[64,4096]{1,0:T(8,128)(2,1)S(1)} all-gather(bf16[64,256]{1,0:T(8,128)(2,1)S(1)} %fusion.66), channel_id=1, replica_groups=mesh['chain'=4,'mesh'=16,'probe'=4] {'mesh'}, dimensions={1}, use_global_device_ids=true | all-gather | bytes 557056 | tf_op jit(solution)/shard_map/while/body/eval_jaxpr/all_gather | solution.py:48
  105.7 0.6 gather_fusion.1
  106.5 41.8 %all_gather.18 = bf16[64,4096]{1,0:T(8,128)(2,1)S(1)} all-gather(bf16[64,256]{1,0:T(8,128)(2,1)S(1)} %fusion.67), channel_id=1, replica_groups=mesh['chain'=4,'mesh'=16,'probe'=4] {'mesh'}, dimensions={1}, use_global_device_ids=true | all-gather | bytes 557056 | tf_op jit(solution)/shard_map/while/body/eval_jaxpr/all_gather | solution.py:44
  148.3 2.3 fusion.68
  150.6 1.3 collective-permute-start
  151.9 0.6 pad_maximum_fusion.2
  152.5 0.2 collective-permute-done
  152.7 44.3 %all_gather.19 = bf16[64,4096]{1,0:T(8,128)(2,1)S(1)} all-gather(bf16[64,256]{1,0:T(8,128)(2,1)S(1)} %collective-permute-done), channel_id=1, replica_groups=mesh['chain'=4,'mesh'=16,'probe'=4] {'mesh'}, dimensions={1}, use_global_device_ids=true | all-gather | bytes 557056 | tf_op jit(solution)/shard_map/while/body/eval_jaxpr/all_gather | solution.py:60
  197.0 0.8 compare_select_fusion.3
  198.1 0.6 gather_fusion
  198.7 1.1 convolution_bitcast_fusion.4
  199.9 41.1 %all_gather.16 = bf16[64,4096]{1,0:T(8,128)(2,1)S(1)} all-gather(bf16[64,256]{1,0:T(8,128)(2,1)S(1)} %fusion.65), channel_id=1, replica_groups=mesh['chain'=4,'mesh'=16,'probe'=4] {'mesh'}, dimensions={1}, use_global_device_ids=true | all-gather | bytes 557056 | tf_op jit(solution)/shard_map/while/body/eval_jaxpr/all_gather | solution.py:44
  241.0 2.3 fusion.66
  243.3 43.2 %all_gather.17 = bf16[64,4096]{1,0:T(8,128)(2,1)S(1)} all-gather(bf16[64,256]{1,0:T(8,128)(2,1)S(1)} %fusion.66), channel_id=1, replica_groups=mesh['chain'=4,'mesh'=16,'probe'=4] {'mesh'}, dimensions={1}, use_global_device_ids=true | all-gather | bytes 557056 | tf_op jit(solution)/shard_map/while/body/eval_jaxpr/all_gather | solution.py:48
  286.7 0.6 gather_fusion.1
  287.5 41.8 %all_gather.18 = bf16[64,4096]{1,0:T(8,128)(2,1)S(1)} all-gather(bf16[64,256]{1,0:T(8,128)(2,1)S(1)} %fusion.67), channel_id=1, replica_groups=mesh['chain'=4,'mesh'=16,'probe'=4] {'mesh'}, dimensions={1}, use_global_device_ids=true | all-gather | bytes 557056 | tf_op jit(solution)/shard_map/while/body/eval_jaxpr/all_gather | solution.py:44
  329.3 2.3 fusion.68
  331.7 1.3 collective-permute-start
  333.0 0.6 pad_maximum_fusion.2
  333.6 0.2 collective-permute-done
  333.8 43.2 %all_gather.19 = bf16[64,4096]{1,0:T(8,128)(2,1)S(1)} all-gather(bf16[64,256]{1,0:T(8,128)(2,1)S(1)} %collective-permute-done), channel_id=1, replica_groups=mesh['chain'=4,'mesh'=16,'probe'=4] {'mesh'}, dimensions={1}, use_global_device_ids=true | all-gather | bytes 557056 | tf_op jit(solution)/shard_map/while/body/eval_jaxpr/all_gather | solution.py:60
  377.0 0.8 compare_select_fusion.3
  378.1 0.6 gather_fusion
  378.7 1.2 convolution_bitcast_fusion.4
  379.9 41.7 %all_gather.16 = bf16[64,4096]{1,0:T(8,128)(2,1)S(1)} all-gather(bf16[64,256]{1,0:T(8,128)(2,1)S(1)} %fusion.65), channel_id=1, replica_groups=mesh['chain'=4,'mesh'=16,'probe'=4] {'mesh'}, dimensions={1}, use_global_device_ids=true | all-gather | bytes 557056 | tf_op jit(solution)/shard_map/while/body/eval_jaxpr/all_gather | solution.py:44
  421.6 2.3 fusion.66
  423.9 43.5 %all_gather.17 = bf16[64,4096]{1,0:T(8,128)(2,1)S(1)} all-gather(bf16[64,256]{1,0:T(8,128)(2,1)S(1)} %fusion.66), channel_id=1, replica_groups=mesh['chain'=4,'mesh'=16,'probe'=4] {'mesh'}, dimensions={1}, use_global_device_ids=true | all-gather | bytes 557056 | tf_op jit(solution)/shard_map/while/body/eval_jaxpr/all_gather | solution.py:48
  467.5 0.6 gather_fusion.1
  468.4 41.9 %all_gather.18 = bf16[64,4096]{1,0:T(8,128)(2,1)S(1)} all-gather(bf16[64,256]{1,0:T(8,128)(2,1)S(1)} %fusion.67), channel_id=1, replica_groups=mesh['chain'=4,'mesh'=16,'probe'=4] {'mesh'}, dimensions={1}, use_global_device_ids=true | all-gather | bytes 557056 | tf_op jit(solution)/shard_map/while/body/eval_jaxpr/all_gather | solution.py:44
  510.3 2.3 fusion.68
  512.6 1.3 collective-permute-start
  513.9 0.6 pad_maximum_fusion.2
  514.6 0.2 collective-permute-done
  514.8 42.1 %all_gather.19 = bf16[64,4096]{1,0:T(8,128)(2,1)S(1)} all-gather(bf16[64,256]{1,0:T(8,128)(2,1)S(1)} %collective-permute-done), channel_id=1, replica_groups=mesh['chain'=4,'mesh'=16,'probe'=4] {'mesh'}, dimensions={1}, use_global_device_ids=true | all-gather | bytes 557056 | tf_op jit(solution)/shard_map/while/body/eval_jaxpr/all_gather | solution.py:60
  556.9 0.8 compare_select_fusion.3
  558.0 0.6 gather_fusion
  558.5 1.1 convolution_bitcast_fusion.4
  559.7 42.6 %all_gather.16 = bf16[64,4096]{1,0:T(8,128)(2,1)S(1)} all-gather(bf16[64,256]{1,0:T(8,128)(2,1)S(1)} %fusion.65), channel_id=1, replica_groups=mesh['chain'=4,'mesh'=16,'probe'=4] {'mesh'}, dimensions={1}, use_global_device_ids=true | all-gather | bytes 557056 | tf_op jit(solution)/shard_map/while/body/eval_jaxpr/all_gather | solution.py:44
  602.4 2.3 fusion.66
  604.7 42.2 %all_gather.17 = bf16[64,4096]{1,0:T(8,128)(2,1)S(1)} all-gather(bf16[64,256]{1,0:T(8,128)(2,1)S(1)} %fusion.66), channel_id=1, replica_groups=mesh['chain'=4,'mesh'=16,'probe'=4] {'mesh'}, dimensions={1}, use_global_device_ids=true | all-gather | bytes 557056 | tf_op jit(solution)/shard_map/while/body/eval_jaxpr/all_gather | solution.py:48
  647.0 0.6 gather_fusion.1
  647.8 42.0 %all_gather.18 = bf16[64,4096]{1,0:T(8,128)(2,1)S(1)} all-gather(bf16[64,256]{1,0:T(8,128)(2,1)S(1)} %fusion.67), channel_id=1, replica_groups=mesh['chain'=4,'mesh'=16,'probe'=4] {'mesh'}, dimensions={1}, use_global_device_ids=true | all-gather | bytes 557056 | tf_op jit(solution)/shard_map/while/body/eval_jaxpr/all_gather | solution.py:44
  689.9 2.3 fusion.68
  692.2 1.3 collective-permute-start
  693.5 0.6 pad_maximum_fusion.2
  694.2 0.2 collective-permute-done
  694.4 42.6 %all_gather.19 = bf16[64,4096]{1,0:T(8,128)(2,1)S(1)} all-gather(bf16[64,256]{1,0:T(8,128)(2,1)S(1)} %collective-permute-done), channel_id=1, replica_groups=mesh['chain'=4,'mesh'=16,'probe'=4] {'mesh'}, dimensions={1}, use_global_device_ids=true | all-gather | bytes 557056 | tf_op jit(solution)/shard_map/while/body/eval_jaxpr/all_gather | solution.py:60
  736.9 1.0 fusion.19
  737.9 1.6 convolution_add_fusion
  739.6 171.2 %all-reduce.4.cloned.1.call-done = f32[64,512]{1,0:T(8,128)} async-done(((f32[64,512]{1,0:T(8,128)}), f32[64,512]{1,0:T(8,128)}) %all-reduce.4.cloned.1.call-update) | async-done | bytes 131088 | tf_op jit(solution)/shard_map/psum | solution.py:76
  910.8 1.5 copy.24
  912.4 0.9 multiply_reduce_fusion.1
  913.2 39.5 %all-reduce.6.cloned.1.call-done = f32[64,512]{1,0:T(8,128)} async-done(((f32[64,512]{1,0:T(8,128)}), f32[64,512]{1,0:T(8,128)}) %all-reduce.6.cloned.1.call-update) | async-done | bytes 131088 | tf_op jit(solution)/shard_map/psum | solution.py:76
  952.7 1.8 multiply_reduce_fusion
  954.6 10.4 %all-reduce = (f32[2,256]{1,0:T(2,128)S(1)}, f32[512]{0:T(512)S(1)}) all-reduce(f32[2,256]{1,0:T(2,128)S(1)} %multiply_reduce_fusion.1, f32[512]{0:T(512)S(1)} %get-tuple-element.71), channel_id=1, replica_groups=mesh['chain'=4,'mesh'=16,'probe'=4] {'probe'}, use_global_device_ids=true, to_apply=%region_5.0 | all-reduce | flops 1024 | bytes 8192 | tf_op jit(solution)/shard_map/psum | solution.py:83
  965.0 0.6 broadcast_multiply_fusion.1
  965.6 0.6 broadcast_multiply_fusion
  (56 shorter events, 2.9 us)
Async XLA Ops:
  7.2 945.6 %copy-start = (bf16[512,512]{1,0:T(8,128)(2,1)S(1)}, bf16[512,512]{1,0:T(8,128)(2,1)}, u32[]{:S(2)}) copy-start(bf16[512,512]{1,0:T(8,128)(2,1)} %param.15) | copy-start | bytes 1572868
  7.2 903.6 %all-reduce.4.cloned.1.call-start = ((), (), s32[]{:S(2)}) async-start(), calls=%async_computation | async-start | bytes 262144 | tf_op jit(solution)/shard_map/psum | solution.py:76
  8.3 728.7 %copy-start.2 = (bf16[2,512,256]{2,1,0:T(8,128)(2,1)S(1)}, bf16[2,512,256]{2,1,0:T(8,128)(2,1)}, u32[]{:S(2)}) copy-start(bf16[2,512,256]{2,1,0:T(8,128)(2,1)} %param.14) | copy-start | bytes 1572868
  8.3 944.5 %copy-start.3 = (s32[64,512]{1,0:T(8,128)S(1)}, s32[64,512]{1,0:T(8,128)}, u32[]{:S(2)}) copy-start(s32[64,512]{1,0:T(8,128)} %param.10) | copy-start | bytes 393220
  8.3 97.9 %copy-start.1 = (bf16[2,2,4,128,128]{4,3,2,1,0:T(8,128)(2,1)S(1)}, bf16[2,2,4,128,128]{4,3,2,1,0:T(8,128)(2,1)}, u32[]{:S(2)}) copy-start(bf16[2,2,4,128,128]{4,3,2,1,0:T(8,128)(2,1)} %get-tuple-element.139) | copy-start | bytes 1572868 | tf_op jit(solution)/shard_map/while
  150.6 2.1 collective-permute-start
  197.0 90.2 %copy-start.1 = (bf16[2,2,4,128,128]{4,3,2,1,0:T(8,128)(2,1)S(1)}, bf16[2,2,4,128,128]{4,3,2,1,0:T(8,128)(2,1)}, u32[]{:S(2)}) copy-start(bf16[2,2,4,128,128]{4,3,2,1,0:T(8,128)(2,1)} %get-tuple-element.139) | copy-start | bytes 1572868 | tf_op jit(solution)/shard_map/while
  331.7 2.1 collective-permute-start
  377.0 91.1 %copy-start.1 = (bf16[2,2,4,128,128]{4,3,2,1,0:T(8,128)(2,1)S(1)}, bf16[2,2,4,128,128]{4,3,2,1,0:T(8,128)(2,1)}, u32[]{:S(2)}) copy-start(bf16[2,2,4,128,128]{4,3,2,1,0:T(8,128)(2,1)} %get-tuple-element.139) | copy-start | bytes 1572868 | tf_op jit(solution)/shard_map/while
  512.6 2.1 collective-permute-start
  556.9 90.7 %copy-start.1 = (bf16[2,2,4,128,128]{4,3,2,1,0:T(8,128)(2,1)S(1)}, bf16[2,2,4,128,128]{4,3,2,1,0:T(8,128)(2,1)}, u32[]{:S(2)}) copy-start(bf16[2,2,4,128,128]{4,3,2,1,0:T(8,128)(2,1)} %get-tuple-element.139) | copy-start | bytes 1572868 | tf_op jit(solution)/shard_map/while
  692.2 2.1 collective-permute-start
  739.6 213.2 %all-reduce.6.cloned.1.call-start = ((), (), s32[]{:S(2)}) async-start(), calls=%async_computation.1 | async-start | bytes 262144 | tf_op jit(solution)/shard_map/psum | solution.py:76
Sparse Core Ops, SparseCore 0:
  739.7 171.0 all-reduce.3
  913.6 39.0 all-reduce.5
where the time goes:
time: 974 us; the launch traced here: 973 us
  blocking collectives  696 us (71%)
  waiting for transfers between devices  212 us (22%)
  matrix products  28.6 us (3%)
  between operations  14.1 us (1%)
    all_gather x8, blocking collectives, sweep(): lax.all_gather(resid_b, 'mesh', axis=1, tiled=True)  338 us
    psum x2, waiting for transfers between devices, shards(): coupled_border = lax.psum(lax.psum(partial_border, 'mesh'), 'chain')  211 us
    all_gather x4, blocking collectives, sweep(): prev = lax.all_gather(solved_now, 'mesh', axis=1, tiled=True)  176 us
    all_gather x4, blocking collectives, turn(): lax.all_gather(as_sent(moved), 'mesh', axis=1, tiled=True)  172 us
  transfers between devices with their start and end apart: 6, of which 6 were waited for; matrix products, arithmetic and copies ran while one was open for 1% of the time, Pallas kernels for 0%

commit v1 on v0

--- a/solution.py
+++ b/solution.py
@@ -41,7 +41,11 @@
         for step in range(steps):
             resid_b = (source[:, step] - coupled_term(prev, step)).astype(jnp.bfloat16)
             solved_now = apply_inverse(
-                inverse_factors[step], lax.all_gather(resid_b, "mesh", axis=1, tiled=True)
+                inverse_factors[step],
+                jnp.concatenate(
+                    lax.all_to_all(jnp.stack([resid_b] * lax.axis_size("mesh")), "mesh", 0, 0),
+                    axis=1,
+                ),
             ).astype(jnp.bfloat16)
             outputs.append(solved_now)
             if step + 1 < steps:

time: 974 us -> 808 us (0.83)
  blocking collectives: 696 us -> 356 us
  waiting for transfers between devices: 212 us -> 314 us
  starting transfers between devices: 5.23 us -> 68.7 us
    all_gather x8 -> x0, blocking collectives: 338 us -> none  [sweep(): lax.all_gather(resid_b, 'mesh', axis=1, tiled=True)]
    all_to_all x0 -> x8, waiting for transfers between devices: none -> 97.7 us  [sweep(): lax.all_to_all(jnp.stack([resid_b] * lax.axis_size('mesh')), 'mesh', 0, 0)]
    all_to_all x0 -> x8, starting transfers between devices: none -> 63.5 us  [sweep(): lax.all_to_all(jnp.stack([resid_b] * lax.axis_size('mesh')), 'mesh', 0, 0)]
  transfers between devices with their start and end apart: 6 -> 14, of which waited for: 6 -> 14; matrix products, arithmetic and copies ran while one was open for 1% -> 1% of each run, Pallas kernels for 0% -> 0%
where the time goes in v1:
time: 808 us; the launch traced here: 806 us
  blocking collectives  356 us (44%)
  waiting for transfers between devices  314 us (39%)
  starting transfers between devices  68.7 us (9%)
  matrix products  28.7 us (4%)
  local copies, waits for them, and re-layouts  15 us (2%)
  between operations  14.1 us (2%)
  other arithmetic  8.52 us (1%)
    psum x2, waiting for transfers between devices, shards(): coupled_border = lax.psum(lax.psum(partial_border, 'mesh'), 'chain')  215 us
    all_gather x4, blocking collectives, sweep(): prev = lax.all_gather(solved_now, 'mesh', axis=1, tiled=True)  174 us
    all_gather x4, blocking collectives, turn(): lax.all_gather(as_sent(moved), 'mesh', axis=1, tiled=True)  172 us
    all_to_all x8, waiting for transfers between devices, sweep(): lax.all_to_all(jnp.stack([resid_b] * lax.axis_size('mesh')), 'mesh', 0, 0)  97.7 us
    all_to_all x8, starting transfers between devices, sweep(): lax.all_to_all(jnp.stack([resid_b] * lax.axis_size('mesh')), 'mesh', 0, 0)  63.5 us
    dot_general x8, matrix products, apply_inverse(): lax.dot_general(piece, factor, (((1,), (1,)), ((), ())), preferred_elemen...  18.8 us
  transfers between devices with their start and end apart: 14, of which 14 were waited for; matrix products, arithmetic and copies ran while one was open for 1% of the time, Pallas kernels for 0%

profile of v1, /device:TPU:8, one launch (start us, length us, event | category | flops | bytes accessed | tf_op | source)
XLA Modules:
  0.0 805.9 jit_solution(7333011538853479896)
XLA Ops:
  7.2 1.0 fusion.24
  8.3 556.9 %while.12 = (s32[]{:T(128)}, bf16[64,4096]{1,0:T(8,128)(2,1)S(1)}, bf16[64,2,256]{2,0,1:T(8,128)(2,1)}, f32[64,2,256]{2,0,1:T(8,128)S(1)}, s32[2,2,4]{2,1,0:T(2,...) while((s32[]{:T(128)}, bf16[64,4096]{1,0:T(8,128)(2,1)S(1)}, ...), condition=%wide.region_1.0_spmd, body=%wide.region_0.0_spmd.sunk | while | flops 302123072 | bytes 19014232 | solution.py:71
  8.3 0.8 compare_select_fusion.3
  9.9 1.2 convolution_bitcast_fusion.4
  11.1 0.8 stack.12
  11.9 11.6 %all-to-all-start = ((bf16[16,64,256]{2,1,0:T(8,128)(2,1)}), bf16[16,64,256]{2,1,0:T(8,128)(2,1)S(1)}, u32[]{:S(2)}, u32[]{:S(2)}) async-start(bf16[16,64,256]{2,1,0:T(8,128)(2,1)} %stack.12), calls=%async_computation | async-start | bytes 1048576 | tf_op jit(solution)/shard_map/while/body/eval_jaxpr/all_to_all | solution.py:46
  23.6 15.6 %all-to-all-done = bf16[16,64,256]{2,1,0:T(8,128)(2,1)S(1)} async-done(((bf16[16,64,256]{2,1,0:T(8,128)(2,1)}), bf16[16,64,256]{2,1,0:T(8,128)(2,1)S(1)}, u32[]{:S(2)}, u32[]{:S(2)}) %all-to-all-start) | async-done | bytes 524320 | tf_op jit(solution)/shard_map/while/body/eval_jaxpr/all_to_all | solution.py:46
  39.2 2.4 fusion.66
  41.5 44.4 %all_gather.8 = bf16[64,4096]{1,0:T(8,128)(2,1)S(1)} all-gather(bf16[64,256]{1,0:T(8,128)(2,1)S(1)} %fusion.66), channel_id=1, replica_groups=mesh['chain'=4,'mesh'=16,'probe'=4] {'mesh'}, dimensions={1}, use_global_device_ids=true | all-gather | bytes 557056 | tf_op jit(solution)/shard_map/while/body/eval_jaxpr/all_gather | solution.py:52
  86.9 0.8 stack.13
  87.7 7.0 all-to-all-start.1
  94.8 12.0 %all-to-all-done.1 = bf16[16,64,256]{2,1,0:T(8,128)(2,1)S(1)} async-done(((bf16[16,64,256]{2,1,0:T(8,128)(2,1)}), bf16[16,64,256]{2,1,0:T(8,128)(2,1)S(1)}, u32[]{:S(2)}, u32[]{:S(2)}) %all-to-all-start.1) | async-done | bytes 524320 | tf_op jit(solution)/shard_map/while/body/eval_jaxpr/all_to_all | solution.py:46
  106.8 2.4 fusion.68
  109.1 1.3 collective-permute-start
  110.4 0.6 pad_maximum_fusion.2
  111.3 42.9 %all_gather.9 = bf16[64,4096]{1,0:T(8,128)(2,1)S(1)} all-gather(bf16[64,256]{1,0:T(8,128)(2,1)S(1)} %collective-permute-done), channel_id=1, replica_groups=mesh['chain'=4,'mesh'=16,'probe'=4] {'mesh'}, dimensions={1}, use_global_device_ids=true | all-gather | bytes 557056 | tf_op jit(solution)/shard_map/while/body/eval_jaxpr/all_gather | solution.py:64
  154.2 0.7 compare_select_fusion.3
  155.7 1.2 convolution_bitcast_fusion.4
  156.9 0.8 stack.12
  157.7 7.9 all-to-all-start
  165.7 10.9 %all-to-all-done = bf16[16,64,256]{2,1,0:T(8,128)(2,1)S(1)} async-done(((bf16[16,64,256]{2,1,0:T(8,128)(2,1)}), bf16[16,64,256]{2,1,0:T(8,128)(2,1)S(1)}, u32[]{:S(2)}, u32[]{:S(2)}) %all-to-all-start) | async-done | bytes 524320 | tf_op jit(solution)/shard_map/while/body/eval_jaxpr/all_to_all | solution.py:46
  176.6 2.4 fusion.66
  179.0 43.8 %all_gather.8 = bf16[64,4096]{1,0:T(8,128)(2,1)S(1)} all-gather(bf16[64,256]{1,0:T(8,128)(2,1)S(1)} %fusion.66), channel_id=1, replica_groups=mesh['chain'=4,'mesh'=16,'probe'=4] {'mesh'}, dimensions={1}, use_global_device_ids=true | all-gather | bytes 557056 | tf_op jit(solution)/shard_map/while/body/eval_jaxpr/all_gather | solution.py:52
  223.7 0.8 stack.13
  224.6 8.2 %all-to-all-start.1 = ((bf16[16,64,256]{2,1,0:T(8,128)(2,1)}), bf16[16,64,256]{2,1,0:T(8,128)(2,1)S(1)}, u32[]{:S(2)}, u32[]{:S(2)}) async-start(bf16[16,64,256]{2,1,0:T(8,128)(2,1)} %stack.13), calls=%async_computation.1 | async-start | bytes 1048576 | tf_op jit(solution)/shard_map/while/body/eval_jaxpr/all_to_all | solution.py:46
  232.8 11.7 %all-to-all-done.1 = bf16[16,64,256]{2,1,0:T(8,128)(2,1)S(1)} async-done(((bf16[16,64,256]{2,1,0:T(8,128)(2,1)}), bf16[16,64,256]{2,1,0:T(8,128)(2,1)S(1)}, u32[]{:S(2)}, u32[]{:S(2)}) %all-to-all-start.1) | async-done | bytes 524320 | tf_op jit(solution)/shard_map/while/body/eval_jaxpr/all_to_all | solution.py:46
  244.6 2.4 fusion.68
  246.9 1.3 collective-permute-start
  248.2 0.6 pad_maximum_fusion.2
  249.1 43.5 %all_gather.9 = bf16[64,4096]{1,0:T(8,128)(2,1)S(1)} all-gather(bf16[64,256]{1,0:T(8,128)(2,1)S(1)} %collective-permute-done), channel_id=1, replica_groups=mesh['chain'=4,'mesh'=16,'probe'=4] {'mesh'}, dimensions={1}, use_global_device_ids=true | all-gather | bytes 557056 | tf_op jit(solution)/shard_map/while/body/eval_jaxpr/all_gather | solution.py:64
  292.6 0.7 compare_select_fusion.3
  294.1 1.2 convolution_bitcast_fusion.4
  295.3 0.8 stack.12
  296.1 5.2 all-to-all-start
  301.4 14.3 %all-to-all-done = bf16[16,64,256]{2,1,0:T(8,128)(2,1)S(1)} async-done(((bf16[16,64,256]{2,1,0:T(8,128)(2,1)}), bf16[16,64,256]{2,1,0:T(8,128)(2,1)S(1)}, u32[]{:S(2)}, u32[]{:S(2)}) %all-to-all-start) | async-done | bytes 524320 | tf_op jit(solution)/shard_map/while/body/eval_jaxpr/all_to_all | solution.py:46
  315.8 2.4 fusion.66
  318.1 42.8 %all_gather.8 = bf16[64,4096]{1,0:T(8,128)(2,1)S(1)} all-gather(bf16[64,256]{1,0:T(8,128)(2,1)S(1)} %fusion.66), channel_id=1, replica_groups=mesh['chain'=4,'mesh'=16,'probe'=4] {'mesh'}, dimensions={1}, use_global_device_ids=true | all-gather | bytes 557056 | tf_op jit(solution)/shard_map/while/body/eval_jaxpr/all_gather | solution.py:52
  361.9 0.8 stack.13
  362.8 6.8 all-to-all-start.1
  369.6 10.8 %all-to-all-done.1 = bf16[16,64,256]{2,1,0:T(8,128)(2,1)S(1)} async-done(((bf16[16,64,256]{2,1,0:T(8,128)(2,1)}), bf16[16,64,256]{2,1,0:T(8,128)(2,1)S(1)}, u32[]{:S(2)}, u32[]{:S(2)}) %all-to-all-start.1) | async-done | bytes 524320 | tf_op jit(solution)/shard_map/while/body/eval_jaxpr/all_to_all | solution.py:46
  380.4 2.4 fusion.68
  382.8 1.3 collective-permute-start
  384.9 42.5 %all_gather.9 = bf16[64,4096]{1,0:T(8,128)(2,1)S(1)} all-gather(bf16[64,256]{1,0:T(8,128)(2,1)S(1)} %collective-permute-done), channel_id=1, replica_groups=mesh['chain'=4,'mesh'=16,'probe'=4] {'mesh'}, dimensions={1}, use_global_device_ids=true | all-gather | bytes 557056 | tf_op jit(solution)/shard_map/while/body/eval_jaxpr/all_gather | solution.py:64
  427.4 0.7 compare_select_fusion.3
  428.9 1.2 convolution_bitcast_fusion.4
  430.1 0.8 stack.12
  431.0 6.8 all-to-all-start
  437.9 11.3 %all-to-all-done = bf16[16,64,256]{2,1,0:T(8,128)(2,1)S(1)} async-done(((bf16[16,64,256]{2,1,0:T(8,128)(2,1)}), bf16[16,64,256]{2,1,0:T(8,128)(2,1)S(1)}, u32[]{:S(2)}, u32[]{:S(2)}) %all-to-all-start) | async-done | bytes 524320 | tf_op jit(solution)/shard_map/while/body/eval_jaxpr/all_to_all | solution.py:46
  449.2 2.4 fusion.66
  451.6 42.9 %all_gather.8 = bf16[64,4096]{1,0:T(8,128)(2,1)S(1)} all-gather(bf16[64,256]{1,0:T(8,128)(2,1)S(1)} %fusion.66), channel_id=1, replica_groups=mesh['chain'=4,'mesh'=16,'probe'=4] {'mesh'}, dimensions={1}, use_global_device_ids=true | all-gather | bytes 557056 | tf_op jit(solution)/shard_map/while/body/eval_jaxpr/all_gather | solution.py:52
  495.5 0.8 stack.13
  496.3 9.9 %all-to-all-start.1 = ((bf16[16,64,256]{2,1,0:T(8,128)(2,1)}), bf16[16,64,256]{2,1,0:T(8,128)(2,1)S(1)}, u32[]{:S(2)}, u32[]{:S(2)}) async-start(bf16[16,64,256]{2,1,0:T(8,128)(2,1)} %stack.13), calls=%async_computation.1 | async-start | bytes 1048576 | tf_op jit(solution)/shard_map/while/body/eval_jaxpr/all_to_all | solution.py:46
  506.2 11.2 %all-to-all-done.1 = bf16[16,64,256]{2,1,0:T(8,128)(2,1)S(1)} async-done(((bf16[16,64,256]{2,1,0:T(8,128)(2,1)}), bf16[16,64,256]{2,1,0:T(8,128)(2,1)S(1)}, u32[]{:S(2)}, u32[]{:S(2)}) %all-to-all-start.1) | async-done | bytes 524320 | tf_op jit(solution)/shard_map/while/body/eval_jaxpr/all_to_all | solution.py:46
  517.4 2.4 fusion.68
  519.8 1.3 collective-permute-start
  521.9 43.2 %all_gather.9 = bf16[64,4096]{1,0:T(8,128)(2,1)S(1)} all-gather(bf16[64,256]{1,0:T(8,128)(2,1)S(1)} %collective-permute-done), channel_id=1, replica_groups=mesh['chain'=4,'mesh'=16,'probe'=4] {'mesh'}, dimensions={1}, use_global_device_ids=true | all-gather | bytes 557056 | tf_op jit(solution)/shard_map/while/body/eval_jaxpr/all_gather | solution.py:64
  565.1 1.0 fusion.19
  566.1 1.6 convolution_add_fusion
  567.8 175.9 %all-reduce.4.cloned.1.call-done = f32[64,512]{1,0:T(8,128)} async-done(((f32[64,512]{1,0:T(8,128)}), f32[64,512]{1,0:T(8,128)}) %all-reduce.4.cloned.1.call-update) | async-done | bytes 131088 | tf_op jit(solution)/shard_map/psum | solution.py:80
  743.8 1.5 copy.32
  745.3 0.9 multiply_reduce_fusion.1
  746.2 39.5 %all-reduce.6.cloned.1.call-done = f32[64,512]{1,0:T(8,128)} async-done(((f32[64,512]{1,0:T(8,128)}), f32[64,512]{1,0:T(8,128)}) %all-reduce.6.cloned.1.call-update) | async-done | bytes 131088 | tf_op jit(solution)/shard_map/psum | solution.py:80
  785.7 1.8 multiply_reduce_fusion
  787.5 10.4 %all-reduce = (f32[2,256]{1,0:T(2,128)S(1)}, f32[512]{0:T(512)S(1)}) all-reduce(f32[2,256]{1,0:T(2,128)S(1)} %multiply_reduce_fusion.1, f32[512]{0:T(512)S(1)} %get-tuple-element.75), channel_id=1, replica_groups=mesh['chain'=4,'mesh'=16,'probe'=4] {'probe'}, use_global_device_ids=true, to_apply=%region_5.0 | all-reduce | flops 1024 | bytes 8192 | tf_op jit(solution)/shard_map/psum | solution.py:87
  (80 shorter events, 11.0 us)
Async XLA Ops:
  7.2 778.5 %copy-start = (bf16[512,512]{1,0:T(8,128)(2,1)S(1)}, bf16[512,512]{1,0:T(8,128)(2,1)}, u32[]{:S(2)}) copy-start(bf16[512,512]{1,0:T(8,128)(2,1)} %param.15) | copy-start | bytes 1572868
  7.2 736.6 %all-reduce.4.cloned.1.call-start = ((), (), s32[]{:S(2)}) async-start(), calls=%async_computation.2 | async-start | bytes 262144 | tf_op jit(solution)/shard_map/psum | solution.py:80
  8.3 556.9 %copy-start.2 = (bf16[2,512,256]{2,1,0:T(8,128)(2,1)S(1)}, bf16[2,512,256]{2,1,0:T(8,128)(2,1)}, u32[]{:S(2)}) copy-start(bf16[2,512,256]{2,1,0:T(8,128)(2,1)} %param.14) | copy-start | bytes 1572868
  8.3 777.4 %copy-start.3 = (s32[64,512]{1,0:T(8,128)S(1)}, s32[64,512]{1,0:T(8,128)}, u32[]{:S(2)}) copy-start(s32[64,512]{1,0:T(8,128)} %param.10) | copy-start | bytes 393220
  9.3 77.3 %copy-start.1 = (bf16[2,2,4,128,128]{4,3,2,1,0:T(8,128)(2,1)S(1)}, bf16[2,2,4,128,128]{4,3,2,1,0:T(8,128)(2,1)}, u32[]{:S(2)}) copy-start(bf16[2,2,4,128,128]{4,3,2,1,0:T(8,128)(2,1)} %get-tuple-element.143) | copy-start | bytes 1572868 | tf_op jit(solution)/shard_map/while
  11.9 27.2 %all-to-all-start = ((bf16[16,64,256]{2,1,0:T(8,128)(2,1)}), bf16[16,64,256]{2,1,0:T(8,128)(2,1)S(1)}, u32[]{:S(2)}, u32[]{:S(2)}) async-start(bf16[16,64,256]{2,1,0:T(8,128)(2,1)} %stack.12), calls=%async_computation | async-start | bytes 1048576 | tf_op jit(solution)/shard_map/while/body/eval_jaxpr/all_to_all | solution.py:46
  87.7 19.0 %all-to-all-start.1 = ((bf16[16,64,256]{2,1,0:T(8,128)(2,1)}), bf16[16,64,256]{2,1,0:T(8,128)(2,1)S(1)}, u32[]{:S(2)}, u32[]{:S(2)}) async-start(bf16[16,64,256]{2,1,0:T(8,128)(2,1)} %stack.13), calls=%async_computation.1 | async-start | bytes 1048576 | tf_op jit(solution)/shard_map/while/body/eval_jaxpr/all_to_all | solution.py:46
  109.1 2.1 collective-permute-start
  155.1 68.4 %copy-start.1 = (bf16[2,2,4,128,128]{4,3,2,1,0:T(8,128)(2,1)S(1)}, bf16[2,2,4,128,128]{4,3,2,1,0:T(8,128)(2,1)}, u32[]{:S(2)}) copy-start(bf16[2,2,4,128,128]{4,3,2,1,0:T(8,128)(2,1)} %get-tuple-element.143) | copy-start | bytes 1572868 | tf_op jit(solution)/shard_map/while
  157.7 18.8 %all-to-all-start = ((bf16[16,64,256]{2,1,0:T(8,128)(2,1)}), bf16[16,64,256]{2,1,0:T(8,128)(2,1)S(1)}, u32[]{:S(2)}, u32[]{:S(2)}) async-start(bf16[16,64,256]{2,1,0:T(8,128)(2,1)} %stack.12), calls=%async_computation | async-start | bytes 1048576 | tf_op jit(solution)/shard_map/while/body/eval_jaxpr/all_to_all | solution.py:46
  224.6 20.0 %all-to-all-start.1 = ((bf16[16,64,256]{2,1,0:T(8,128)(2,1)}), bf16[16,64,256]{2,1,0:T(8,128)(2,1)S(1)}, u32[]{:S(2)}, u32[]{:S(2)}) async-start(bf16[16,64,256]{2,1,0:T(8,128)(2,1)} %stack.13), calls=%async_computation.1 | async-start | bytes 1048576 | tf_op jit(solution)/shard_map/while/body/eval_jaxpr/all_to_all | solution.py:46
  246.9 2.1 collective-permute-start
  293.5 68.2 %copy-start.1 = (bf16[2,2,4,128,128]{4,3,2,1,0:T(8,128)(2,1)S(1)}, bf16[2,2,4,128,128]{4,3,2,1,0:T(8,128)(2,1)}, u32[]{:S(2)}) copy-start(bf16[2,2,4,128,128]{4,3,2,1,0:T(8,128)(2,1)} %get-tuple-element.143) | copy-start | bytes 1572868 | tf_op jit(solution)/shard_map/while
  296.1 19.6 %all-to-all-start = ((bf16[16,64,256]{2,1,0:T(8,128)(2,1)}), bf16[16,64,256]{2,1,0:T(8,128)(2,1)S(1)}, u32[]{:S(2)}, u32[]{:S(2)}) async-start(bf16[16,64,256]{2,1,0:T(8,128)(2,1)} %stack.12), calls=%async_computation | async-start | bytes 1048576 | tf_op jit(solution)/shard_map/while/body/eval_jaxpr/all_to_all | solution.py:46
  362.8 17.6 %all-to-all-start.1 = ((bf16[16,64,256]{2,1,0:T(8,128)(2,1)}), bf16[16,64,256]{2,1,0:T(8,128)(2,1)S(1)}, u32[]{:S(2)}, u32[]{:S(2)}) async-start(bf16[16,64,256]{2,1,0:T(8,128)(2,1)} %stack.13), calls=%async_computation.1 | async-start | bytes 1048576 | tf_op jit(solution)/shard_map/while/body/eval_jaxpr/all_to_all | solution.py:46
  382.8 2.1 collective-permute-start
  428.4 66.9 %copy-start.1 = (bf16[2,2,4,128,128]{4,3,2,1,0:T(8,128)(2,1)S(1)}, bf16[2,2,4,128,128]{4,3,2,1,0:T(8,128)(2,1)}, u32[]{:S(2)}) copy-start(bf16[2,2,4,128,128]{4,3,2,1,0:T(8,128)(2,1)} %get-tuple-element.143) | copy-start | bytes 1572868 | tf_op jit(solution)/shard_map/while
  431.0 18.2 %all-to-all-start = ((bf16[16,64,256]{2,1,0:T(8,128)(2,1)}), bf16[16,64,256]{2,1,0:T(8,128)(2,1)S(1)}, u32[]{:S(2)}, u32[]{:S(2)}) async-start(bf16[16,64,256]{2,1,0:T(8,128)(2,1)} %stack.12), calls=%async_computation | async-start | bytes 1048576 | tf_op jit(solution)/shard_map/while/body/eval_jaxpr/all_to_all | solution.py:46
  496.3 21.1 %all-to-all-start.1 = ((bf16[16,64,256]{2,1,0:T(8,128)(2,1)}), bf16[16,64,256]{2,1,0:T(8,128)(2,1)S(1)}, u32[]{:S(2)}, u32[]{:S(2)}) async-start(bf16[16,64,256]{2,1,0:T(8,128)(2,1)} %stack.13), calls=%async_computation.1 | async-start | bytes 1048576 | tf_op jit(solution)/shard_map/while/body/eval_jaxpr/all_to_all | solution.py:46
  519.8 2.1 collective-permute-start
  567.7 217.9 %all-reduce.6.cloned.1.call-start = ((), (), s32[]{:S(2)}) async-start(), calls=%async_computation.3 | async-start | bytes 262144 | tf_op jit(solution)/shard_map/psum | solution.py:80
Sparse Core Ops, SparseCore 0:
  567.9 175.8 all-reduce.3
  746.5 39.0 all-reduce.5
